TPU v7x, 32 devices: a whole 2x2x4 slice. The times are simulated.
32 devices in a mesh: lon: 8 (over y, x, core), lat: 4 (over z).
Axes of the slice: x: 2, y: 2, z: 4, core: 2. Of those that a mesh axis runs over, the one named last changes fastest.
Arguments:
- fields: float32 [5, 1, 128, 11520], P(None, None, 'lat', 'lon'), may hold values from -6 to 6
- frac_x: float32 [2, 1, 128], replicated, may hold values from 0.05 to 0.95
- frac_y: float32 [2, 1, 128], replicated, may hold values from 0.05 to 0.9
- shift_cells: int32 [2, 1, 128], replicated, may hold values from -5760 to 5759, as said below
- polar_mask: int32 [128], replicated, may hold values from 0 to 1, as said below
Outputs:
- fields_out: float32 [5, 1, 128, 11520], P(None, None, 'lat', 'lon')
Inputs may be any that keep to these rules, and one draw needn't show every extreme that they name: `shift_cells`: outside the first and last 32 rows every count lies in -2 .. 1, and both -2 and 1 occur there. `polar_mask`: nonzero only in the first and last 32 rows; the first and the last row are 1.
All inputs are finite; a program needn't handle non-finite values.
Results may differ from a plain program's by a relative error of at most 0.00016.
Values sent between devices are 32-bit elements; how exact they have to be, the bound alone decides.
A program may use at most 64 MiB of HBM per device.

v0:
```python
import math
import jax
import jax.numpy as jnp
from jax import lax
from jax.sharding import PartitionSpec as P

FA = 90
FB = 128
SUBS = 2
REACH = 4


def passed_along(x, axis, by):
    devices = lax.axis_size(axis)
    return lax.ppermute(x, axis, [(i, (i + by) % devices) for i in range(devices)])


def passed_along_2(block, axis, distance):
    devices = range(lax.axis_size(axis))
    route = [(i - distance, i) for i in devices if i - distance in devices]
    return lax.ppermute(block, axis, route)


def roll_digits(values, amount, span, axis):
    bit_total = max((span - 1).bit_length(), 1)
    for bit in range(bit_total):
        moved = jnp.roll(values, 1 << bit, axis=axis)
        taken = amount >> bit & 1 == 1
        values = jnp.where(taken, moved, values)
    return values


def cycle_move(state, counts, lon_cells):
    device_jump = jnp.floor_divide(counts, lon_cells)
    remainder = counts - device_jump * lon_cells
    select = device_jump + REACH
    bit_count = (2 * REACH).bit_length() - 1
    offsets = [-REACH] + [1 << bit for bit in range(bit_count)]
    current = state
    for turn, offset in enumerate(offsets):
        moved = passed_along(current, "lon", offset)
        if turn == 0:
            current = moved
        else:
            taken = select >> turn - 1 & 1 == 1
            current = jnp.where(taken[None, :, :, None], moved, current)
    western = passed_along(current, "lon", 1)
    joined = jnp.concatenate([western, current], axis=3)
    rolled = roll_digits(joined, remainder[None, :, :, None], lon_cells, 3)
    return rolled[:, :, :, lon_cells:]


def zonal_fraction(whole, courant):
    previous = jnp.roll(whole, 1, axis=1)
    edge = whole + 0.5 * (1.0 - courant) * (whole - previous)
    return whole - courant * (edge - jnp.roll(edge, 1, axis=1))


def polar_smooth(whole, lat_rows, marks, lat_cells, lat_total):
    row_count, lon_total = whole.shape
    highest = lax.Precision.HIGHEST
    first_ids = jnp.arange(FA, dtype=jnp.int32)
    second_ids = jnp.arange(FB, dtype=jnp.int32)
    angle_first = (
        2.0 * math.pi * (first_ids[:, None] * first_ids[None, :] % FA).astype(jnp.float32) / FA
    )
    cos_first, sin_first = (jnp.cos(angle_first), jnp.sin(angle_first))
    angle_second = (
        2.0 * math.pi * (second_ids[:, None] * second_ids[None, :] % FB).astype(jnp.float32) / FB
    )
    cos_second, sin_second = (jnp.cos(angle_second), jnp.sin(angle_second))
    angle_twist = (
        2.0
        * math.pi
        * (first_ids[:, None] * second_ids[None, :] % lon_total).astype(jnp.float32)
        / lon_total
    )
    cos_twist, sin_twist = (jnp.cos(angle_twist), jnp.sin(angle_twist))
    waves = (first_ids[:, None] + FA * second_ids[None, :]).astype(jnp.float32)
    sine = jnp.sin(math.pi * waves / lon_total)
    phi = math.pi * (lat_rows.astype(jnp.float32) + 0.5) / lat_total - math.pi / 2
    edge_cos = math.sin(math.pi * (lat_cells - 0.5) / lat_total)
    b_val = jnp.cos(phi) / edge_cos
    gain = 1.0 / (1.0 + sine[None, :, :] ** 2 / b_val[:, None, None] ** 2)
    grid = whole.reshape(row_count, FA, FB)
    real_one = jnp.einsum("kn,rnm->rkm", cos_first, grid, precision=highest)
    imag_one = -jnp.einsum("kn,rnm->rkm", sin_first, grid, precision=highest)
    real_two = real_one * cos_twist + imag_one * sin_twist
    imag_two = imag_one * cos_twist - real_one * sin_twist
    real_spec = jnp.einsum("rkm,mq->rkq", real_two, cos_second, precision=highest) + jnp.einsum(
        "rkm,mq->rkq", imag_two, sin_second, precision=highest
    )
    imag_spec = jnp.einsum("rkm,mq->rkq", imag_two, cos_second, precision=highest) - jnp.einsum(
        "rkm,mq->rkq", real_two, sin_second, precision=highest
    )
    real_spec = real_spec * gain
    imag_spec = imag_spec * gain
    real_back = jnp.einsum("rkq,mq->rkm", real_spec, cos_second, precision=highest) - jnp.einsum(
        "rkq,mq->rkm", imag_spec, sin_second, precision=highest
    )
    imag_back = jnp.einsum("rkq,mq->rkm", imag_spec, cos_second, precision=highest) + jnp.einsum(
        "rkq,mq->rkm", real_spec, sin_second, precision=highest
    )
    real_turn = real_back * cos_twist - imag_back * sin_twist
    imag_turn = imag_back * cos_twist + real_back * sin_twist
    result = jnp.einsum("kn,rkm->rnm", cos_first, real_turn, precision=highest) - jnp.einsum(
        "kn,rkm->rnm", sin_first, imag_turn, precision=highest
    )
    result = result.reshape(row_count, lon_total) / lon_total
    return jnp.where((marks == 1)[:, None], result, whole)


def meridional(state, merid_step, first_row):
    n_fields, n_levels, lat_cells, lon_cells = state.shape
    southern = passed_along_2(state[:, :, lat_cells - 2 :, :], "lat", 1)
    extended = jnp.concatenate([southern, state], axis=2)
    padded_faces = jnp.concatenate([merid_step, jnp.zeros((n_levels, 1), jnp.float32)], axis=1)
    faces = lax.dynamic_slice_in_dim(padded_faces, first_row, lat_cells + 1, 1)
    face_ids = first_row + jnp.arange(lat_cells + 1, dtype=jnp.int32)
    faces = jnp.where((face_ids == 0)[None, :], jnp.zeros_like(faces), faces)
    courant = faces[None, :, :, None]
    upper = extended[:, :, 1 : lat_cells + 2, :]
    lower = extended[:, :, 0 : lat_cells + 1, :]
    flux = courant * (upper + 0.5 * (1.0 - courant) * (upper - lower))
    return state + flux[:, :, :lat_cells, :] - flux[:, :, 1:, :]


def body(fields, frac_x, frac_y, shift_cells, polar_mask):
    n_fields, n_levels, lat_cells, lon_cells = fields.shape
    lon_devs = lax.axis_size("lon")
    lat_total = lat_cells * lax.axis_size("lat")
    lon_index = lax.axis_index("lon")
    first_row = lax.axis_index("lat") * lat_cells
    row_total = n_fields * n_levels * lat_cells
    per_device = row_total // lon_devs
    row_start = lon_index * per_device
    local_rows = first_row + jnp.arange(lat_cells, dtype=jnp.int32)
    marks_local = lax.dynamic_slice_in_dim(polar_mask, first_row, lat_cells, 0)

    def my_rows(table):
        spread = jnp.broadcast_to(table[None], (n_fields, n_levels, lat_cells)).reshape(row_total)
        return lax.dynamic_slice_in_dim(spread, row_start, per_device, 0)

    row_lats = my_rows(local_rows[None])
    row_marks = my_rows(marks_local[None])
    state = fields
    for substep in range(SUBS):
        counts = lax.dynamic_slice_in_dim(shift_cells[substep], first_row, lat_cells, 1)
        fractions = lax.dynamic_slice_in_dim(frac_x[substep], first_row, lat_cells, 1)
        placed = cycle_move(state, counts, lon_cells)
        flat = placed.reshape(row_total, lon_cells)
        whole = lax.all_to_all(flat, "lon", split_axis=0, concat_axis=1, tiled=True)
        whole = zonal_fraction(whole, my_rows(fractions)[:, None])
        whole = polar_smooth(whole, row_lats, row_marks, lat_cells, lat_total)
        blocks = lax.all_to_all(whole, "lon", split_axis=1, concat_axis=0, tiled=True)
        state = blocks.reshape(n_fields, n_levels, lat_cells, lon_cells)
        state = meridional(state, frac_y[substep], first_row)
    return state


def solution(mesh):
    return jax.shard_map(
        body,
        mesh=mesh,
        in_specs=(P(None, None, "lat", "lon"), P(), P(), P(), P()),
        out_specs=P(None, None, "lat", "lon"),
        check_vma=False,
    )
```

profile of v0, /device:TPU:0, one launch (start us, length us, event | category | flops | bytes accessed | tf_op | source)
XLA Modules:
  0.0 374.6 jit_solution(14722888508883360047)
XLA Ops:
  0.0 3.0 collective-permute-start
  3.0 22.0 %collective-permute-done = f32[5,1,32,1440]{3,2,1,0:T(8,128)S(1)} collective-permute-done((f32[5,1,32,1440]{3,2,1,0:T(8,128)}, f32[5,1,32,1440]{3,2,1,0:T(8,128)S(1)}, u32[]{:S(2)}, u32[]{:S(2)}) %collective-permute-start) | collective-permute-done | bytes 921632 | tf_op jit(solution)/shard_map/ppermute | solution.py:15
  26.3 13.1 %collective-permute-done.1 = f32[5,1,32,1440]{3,2,1,0:T(8,128)S(1)} collective-permute-done((f32[5,1,32,1440]{3,2,1,0:T(8,128)S(1)}, f32[5,1,32,1440]{3,2,1,0:T(8,128)S(1)}, u32[]{:S(2)}, u32[]{:S(2)}) %collective-permute-start.1) | collective-permute-done | bytes 921632 | tf_op jit(solution)/shard_map/ppermute | solution.py:15
  40.4 22.2 %collective-permute-done.2 = f32[5,1,32,1440]{3,2,1,0:T(8,128)S(1)} collective-permute-done((f32[5,1,32,1440]{3,2,1,0:T(8,128)S(1)}, f32[5,1,32,1440]{3,2,1,0:T(8,128)S(1)}, u32[]{:S(2)}, u32[]{:S(2)}) %collective-permute-start.2) | collective-permute-done | bytes 921632 | tf_op jit(solution)/shard_map/ppermute | solution.py:15
  62.8 1.6 collective-permute-start.3
  64.4 19.7 %collective-permute-done.3 = f32[5,1,32,1440]{3,2,1,0:T(8,128)S(1)} collective-permute-done((f32[5,1,32,1440]{3,2,1,0:T(8,128)S(1)}, f32[5,1,32,1440]{3,2,1,0:T(8,128)S(1)}, u32[]{:S(2)}, u32[]{:S(2)}) %collective-permute-start.3) | collective-permute-done | bytes 921632 | tf_op jit(solution)/shard_map/ppermute | solution.py:15
  85.2 13.6 %collective-permute-done.4 = f32[5,1,32,1440]{3,2,1,0:T(8,128)S(1)} collective-permute-done((f32[5,1,32,1440]{3,2,1,0:T(8,128)S(1)}, f32[5,1,32,1440]{3,2,1,0:T(8,128)S(1)}, u32[]{:S(2)}, u32[]{:S(2)}) %collective-permute-start.4) | collective-permute-done | bytes 921632 | tf_op jit(solution)/shard_map/ppermute | solution.py:15
  106.3 1.2 all_to_all.52
  107.5 3.8 %all-to-all-start = ((f32[8,20,1440]{2,1,0:T(8,128)}), f32[8,20,1440]{2,1,0:T(8,128)S(1)}, u32[]{:S(2)}, u32[]{:S(2)}) async-start(f32[8,20,1440]{2,1,0:T(8,128)} %all_to_all.52), calls=%async_computation | async-start | bytes 2359296 | tf_op jit(solution)/shard_map/all_to_all | solution.py:152
  112.8 15.0 %all-to-all-done = f32[8,20,1440]{2,1,0:T(8,128)S(1)} async-done(((f32[8,20,1440]{2,1,0:T(8,128)}), f32[8,20,1440]{2,1,0:T(8,128)S(1)}, u32[]{:S(2)}, u32[]{:S(2)}) %all-to-all-start) | async-done | bytes 921632 | tf_op jit(solution)/shard_map/all_to_all | solution.py:152
  128.4 1.4 all_to_all.55
  131.2 1.6 concatenate.853
  132.9 1.2 concatenate.851
  134.1 1.6 concatenate.852
  136.8 2.1 multiply_subtract_fusion.3
  138.9 1.2 fusion.13
  140.1 1.2 convolution_bitcast_fusion.1
  141.3 1.2 fusion.55
  142.5 1.2 fusion.54
  143.7 1.2 fusion.11
  144.9 1.6 fusion.75
  146.5 1.2 fusion.12
  147.7 1.2 fusion.78
  148.8 1.2 convolution_add_fusion.2
  150.0 1.2 convolution_subtract_fusion.4
  151.2 1.3 fusion.42
  152.5 2.3 fusion.10
  154.8 2.9 div.293
  157.7 4.0 %copy_select_fusion.1 = f32[20,8,1440]{2,0,1:T(8,128)} fusion(f32[20,8,1440]{2,1,0:T(8,128)} %div.293, f32[20,8,1440]{2,1,0:T(8,128)S(1)} %copy-done.2, f32[20,8,1440]{2,1,0:T(8,128)S(1)} %copy-done.3, f32[20]{0:T(128)S(1)} %get-tuple-element.18, f32[20]{0:T(128)S(1)} %get-tuple-element.19, pred[20]{0:T(512)(128)(4,1)S(1)} %dynamic-slice_compare_fusion, ...), kind=kLoop, calls=%fused_computation.69 | loop fusion | flops 1612800 | bytes 4608180 | tf_op jit(solution)/shard_map/jit(_where)/select_n | solution.py:110
  161.7 3.7 all-to-all-start.1
  166.0 16.2 %all-to-all-done.1 = f32[20,8,1440]{2,0,1:T(8,128)S(1)} async-done(((f32[20,8,1440]{2,0,1:T(8,128)}), f32[20,8,1440]{2,0,1:T(8,128)S(1)}, u32[]{:S(2)}, u32[]{:S(2)}) %all-to-all-start.1) | async-done | bytes 921632 | tf_op jit(solution)/shard_map/all_to_all | solution.py:155
  182.3 3.3 collective-permute-start.5
  185.6 1.8 collective-permute-done.5
  188.6 19.2 %collective-permute-done.6 = f32[5,1,32,1440]{3,2,0,1:T(8,128)S(1)} collective-permute-done((f32[5,1,32,1440]{3,2,0,1:T(8,128)S(1)}, f32[5,1,32,1440]{3,2,0,1:T(8,128)S(1)}, u32[]{:S(2)}, u32[]{:S(2)}) %collective-permute-start.6) | collective-permute-done | bytes 921632 | tf_op jit(solution)/shard_map/ppermute | solution.py:15
  207.9 14.4 %collective-permute-done.7 = f32[5,1,32,1440]{3,2,0,1:T(8,128)S(1)} collective-permute-done((f32[5,1,32,1440]{3,2,0,1:T(8,128)S(1)}, f32[5,1,32,1440]{3,2,0,1:T(8,128)S(1)}, u32[]{:S(2)}, u32[]{:S(2)}) %collective-permute-start.7) | collective-permute-done | bytes 921632 | tf_op jit(solution)/shard_map/ppermute | solution.py:15
  222.5 2.9 collective-permute-start.8
  225.4 22.2 %collective-permute-done.8 = f32[5,1,32,1440]{3,2,0,1:T(8,128)S(1)} collective-permute-done((f32[5,1,32,1440]{3,2,0,1:T(8,128)S(1)}, f32[5,1,32,1440]{3,2,0,1:T(8,128)S(1)}, u32[]{:S(2)}, u32[]{:S(2)}) %collective-permute-start.8) | collective-permute-done | bytes 921632 | tf_op jit(solution)/shard_map/ppermute | solution.py:15
  248.2 22.8 %collective-permute-done.9 = f32[5,1,32,1440]{3,2,0,1:T(8,128)S(1)} collective-permute-done((f32[5,1,32,1440]{3,2,0,1:T(8,128)S(1)}, f32[5,1,32,1440]{3,2,0,1:T(8,128)S(1)}, u32[]{:S(2)}, u32[]{:S(2)}) %collective-permute-start.9) | collective-permute-done | bytes 921632 | tf_op jit(solution)/shard_map/ppermute | solution.py:15
  271.4 14.3 %collective-permute-done.10 = f32[5,1,32,1440]{3,2,0,1:T(8,128)S(1)} collective-permute-done((f32[5,1,32,1440]{3,2,0,1:T(8,128)S(1)}, f32[5,1,32,1440]{3,2,0,1:T(8,128)S(1)}, u32[]{:S(2)}, u32[]{:S(2)}) %collective-permute-start.10) | collective-permute-done | bytes 921632 | tf_op jit(solution)/shard_map/ppermute | solution.py:15
  293.3 1.2 all_to_all.59
  294.5 3.8 %all-to-all-start.2 = ((f32[8,20,1440]{2,1,0:T(8,128)}), f32[8,20,1440]{2,1,0:T(8,128)S(1)}, u32[]{:S(2)}, u32[]{:S(2)}) async-start(f32[8,20,1440]{2,1,0:T(8,128)} %all_to_all.59), calls=%async_computation.2 | async-start | bytes 2359296 | tf_op jit(solution)/shard_map/all_to_all | solution.py:152
  298.4 16.3 %all-to-all-done.2 = f32[8,20,1440]{2,1,0:T(8,128)S(1)} async-done(((f32[8,20,1440]{2,1,0:T(8,128)}), f32[8,20,1440]{2,1,0:T(8,128)S(1)}, u32[]{:S(2)}, u32[]{:S(2)}) %all-to-all-start.2) | async-done | bytes 921632 | tf_op jit(solution)/shard_map/all_to_all | solution.py:152
  315.3 1.4 all_to_all.62
  318.2 1.6 concatenate.873
  319.8 1.2 concatenate.871
  321.0 1.6 concatenate.872
  323.8 2.1 multiply_subtract_fusion.1
  325.9 1.2 fusion.8
  327.0 1.2 convolution_bitcast_fusion
  328.2 1.2 fusion.57
  329.4 1.2 fusion.56
  330.6 1.2 fusion.6
  331.8 1.2 fusion.69
  333.0 1.4 fusion.7
  334.4 1.2 fusion.72
  335.6 1.2 convolution_add_fusion
  336.8 1.2 convolution_subtract_fusion.1
  338.0 1.3 fusion.35
  339.3 2.3 fusion.5
  341.6 2.9 div.296
  344.5 2.9 copy_select_fusion
  347.5 19.2 %all_to_all.70 = f32[20,8,1440]{2,0,1:T(8,128)S(1)} all-to-all(f32[20,8,1440]{2,0,1:T(8,128)S(1)} %copy_select_fusion), channel_id=1, replica_groups=mesh['lon'=8,'lat'=4] {'lon'}, dimensions={1} | all-to-all | bytes 1843200 | tf_op jit(solution)/shard_map/all_to_all | solution.py:155
  366.8 4.0 %collective-permute-start.11 = (f32[5,1,2,1440]{3,2,0,1:T(2,128)S(1)}, f32[5,1,2,1440]{3,2,0,1:T(2,128)S(1)}, u32[]{:S(2)}, u32[]{:S(2)}) collective-permute-start(f32[5,1,2,1440]{3,2,0,1:T(2,128)S(1)} %slice.367), channel_id=1, source_target_pairs={{0,1},{1,2},{2,3},{4,5},{5,6},{6,7},{8,9},{9,10},{10,11},{12,13},{... | collective-permute-start | bytes 172808 | tf_op jit(solution)/shard_map/ppermute | solution.py:21
  370.8 1.8 collective-permute-done.11
  (148 shorter events, 31.3 us)
Async XLA Ops:
  0.0 24.9 %collective-permute-start = (f32[5,1,32,1440]{3,2,1,0:T(8,128)}, f32[5,1,32,1440]{3,2,1,0:T(8,128)S(1)}, u32[]{:S(2)}, u32[]{:S(2)}) collective-permute-start(f32[5,1,32,1440]{3,2,1,0:T(8,128)} %param.5), channel_id=1, source_target_pairs={{0,16},{4,20},{8,24},{12,28},{16,0},{20,4},{24,8},{28,12},{1,17},{... | collective-permute-start | bytes 2764808 | tf_op jit(solution)/shard_map/ppermute | solution.py:15
  24.9 14.4 %collective-permute-start.1 = (f32[5,1,32,1440]{3,2,1,0:T(8,128)S(1)}, f32[5,1,32,1440]{3,2,1,0:T(8,128)S(1)}, u32[]{:S(2)}, u32[]{:S(2)}) collective-permute-start(f32[5,1,32,1440]{3,2,1,0:T(8,128)S(1)} %collective-permute-done), channel_id=1, source_target_pairs={{0,4},{4,8},{8,12},{12,16},{16,20},{20,24},{24,28},{28,0},{1,5},{5... | collective-permute-start | bytes 2764808 | tf_op jit(solution)/shard_map/ppermute | solution.py:15
  39.6 23.1 %collective-permute-start.2 = (f32[5,1,32,1440]{3,2,1,0:T(8,128)S(1)}, f32[5,1,32,1440]{3,2,1,0:T(8,128)S(1)}, u32[]{:S(2)}, u32[]{:S(2)}) collective-permute-start(f32[5,1,32,1440]{3,2,1,0:T(8,128)S(1)} %broadcast_select_fusion), channel_id=1, source_target_pairs={{0,8},{4,12},{8,16},{12,20},{16,24},{20,28},{24,0},{28,4},{1,9},{5... | collective-permute-start | bytes 2764808 | tf_op jit(solution)/shard_map/ppermute | solution.py:15
  62.8 21.5 %copy-start.12 = (s32[128]{0:T(128)S(1)}, s32[128]{0:T(128)}, u32[]{:S(2)}) copy-start(s32[128]{0:T(128)} %param.9) | copy-start | bytes 1540
  62.8 21.6 %copy-start.10 = (f32[2,1,128]{2,1,0:T(1,128)S(1)}, f32[2,1,128]{2,1,0:T(1,128)}, u32[]{:S(2)}) copy-start(f32[2,1,128]{2,1,0:T(1,128)} %param.6) | copy-start | bytes 3076
  62.8 21.3 %collective-permute-start.3 = (f32[5,1,32,1440]{3,2,1,0:T(8,128)S(1)}, f32[5,1,32,1440]{3,2,1,0:T(8,128)S(1)}, u32[]{:S(2)}, u32[]{:S(2)}) collective-permute-start(f32[5,1,32,1440]{3,2,1,0:T(8,128)S(1)} %broadcast_select_fusion.1), channel_id=1, source_target_pairs={{0,16},{4,20},{8,24},{12,28},{16,0},{20,4},{24,8},{28,12},{1,17},{... | collective-permute-start | bytes 2764808 | tf_op jit(solution)/shard_map/ppermute | solution.py:15
  84.3 14.5 %collective-permute-start.4 = (f32[5,1,32,1440]{3,2,1,0:T(8,128)S(1)}, f32[5,1,32,1440]{3,2,1,0:T(8,128)S(1)}, u32[]{:S(2)}, u32[]{:S(2)}) collective-permute-start(f32[5,1,32,1440]{3,2,1,0:T(8,128)S(1)} %broadcast_select_fusion.2), channel_id=1, source_target_pairs={{0,4},{4,8},{8,12},{12,16},{16,20},{20,24},{24,28},{28,0},{1,5},{5... | collective-permute-start | bytes 2764808 | tf_op jit(solution)/shard_map/ppermute | solution.py:15
  107.5 20.3 %all-to-all-start = ((f32[8,20,1440]{2,1,0:T(8,128)}), f32[8,20,1440]{2,1,0:T(8,128)S(1)}, u32[]{:S(2)}, u32[]{:S(2)}) async-start(f32[8,20,1440]{2,1,0:T(8,128)} %all_to_all.52), calls=%async_computation | async-start | bytes 2359296 | tf_op jit(solution)/shard_map/all_to_all | solution.py:152
  134.0 2.8 copy-start.4
  142.4 1.2 copy-start.13
  154.8 2.9 copy-start.2
  154.8 2.9 copy-start.3
  161.7 3.7 copy-start.11
  161.7 20.4 %all-to-all-start.1 = ((f32[20,8,1440]{2,0,1:T(8,128)}), f32[20,8,1440]{2,0,1:T(8,128)S(1)}, u32[]{:S(2)}, u32[]{:S(2)}) async-start(f32[20,8,1440]{2,0,1:T(8,128)} %copy_select_fusion.1), calls=%async_computation.1 | async-start | bytes 2359296 | tf_op jit(solution)/shard_map/all_to_all | solution.py:155
  182.3 5.1 %collective-permute-start.5 = (f32[5,1,2,1440]{3,2,0,1:T(2,128)S(1)}, f32[5,1,2,1440]{3,2,0,1:T(2,128)S(1)}, u32[]{:S(2)}, u32[]{:S(2)}) collective-permute-start(f32[5,1,2,1440]{3,2,0,1:T(2,128)S(1)} %slice.334), channel_id=1, source_target_pairs={{0,1},{1,2},{2,3},{4,5},{5,6},{6,7},{8,9},{9,10},{10,11},{12,13},{... | collective-permute-start | bytes 172808 | tf_op jit(solution)/shard_map/ppermute | solution.py:21
  187.8 20.1 %copy-start.7 = (s32[32]{0:T(128)S(1)}, s32[32]{0:T(128)}, u32[]{:S(2)}) copy-start(s32[32]{0:T(128)} %get-tuple-element.57) | copy-start | bytes 388
  188.0 19.8 %collective-permute-start.6 = (f32[5,1,32,1440]{3,2,0,1:T(8,128)S(1)}, f32[5,1,32,1440]{3,2,0,1:T(8,128)S(1)}, u32[]{:S(2)}, u32[]{:S(2)}) collective-permute-start(f32[5,1,32,1440]{3,2,0,1:T(8,128)S(1)} %slice_subtract_fusion.1), channel_id=1, source_target_pairs={{0,16},{4,20},{8,24},{12,28},{16,0},{20,4},{24,8},{28,12},{1,17},{... | collective-permute-start | bytes 2764808 | tf_op jit(solution)/shard_map/ppermute | solution.py:15
  207.9 14.4 %collective-permute-start.7 = (f32[5,1,32,1440]{3,2,0,1:T(8,128)S(1)}, f32[5,1,32,1440]{3,2,0,1:T(8,128)S(1)}, u32[]{:S(2)}, u32[]{:S(2)}) collective-permute-start(f32[5,1,32,1440]{3,2,0,1:T(8,128)S(1)} %collective-permute-done.6), channel_id=1, source_target_pairs={{0,4},{4,8},{8,12},{12,16},{16,20},{20,24},{24,28},{28,0},{1,5},{5... | collective-permute-start | bytes 2764808 | tf_op jit(solution)/shard_map/ppermute | solution.py:15
  222.5 25.1 %collective-permute-start.8 = (f32[5,1,32,1440]{3,2,0,1:T(8,128)S(1)}, f32[5,1,32,1440]{3,2,0,1:T(8,128)S(1)}, u32[]{:S(2)}, u32[]{:S(2)}) collective-permute-start(f32[5,1,32,1440]{3,2,0,1:T(8,128)S(1)} %broadcast_select_fusion.3), channel_id=1, source_target_pairs={{0,8},{4,12},{8,16},{12,20},{16,24},{20,28},{24,0},{28,4},{1,9},{5... | collective-permute-start | bytes 2764808 | tf_op jit(solution)/shard_map/ppermute | solution.py:15
  247.8 23.5 %copy-start.8 = (s32[32]{0:T(128)S(1)}, s32[32]{0:T(128)}, u32[]{:S(2)}) copy-start(s32[32]{0:T(128)} %get-tuple-element.56) | copy-start | bytes 388
  247.8 23.3 %collective-permute-start.9 = (f32[5,1,32,1440]{3,2,0,1:T(8,128)S(1)}, f32[5,1,32,1440]{3,2,0,1:T(8,128)S(1)}, u32[]{:S(2)}, u32[]{:S(2)}) collective-permute-start(f32[5,1,32,1440]{3,2,0,1:T(8,128)S(1)} %broadcast_select_fusion.4), channel_id=1, source_target_pairs={{0,16},{4,20},{8,24},{12,28},{16,0},{20,4},{24,8},{28,12},{1,17},{... | collective-permute-start | bytes 2764808 | tf_op jit(solution)/shard_map/ppermute | solution.py:15
  271.3 14.5 %collective-permute-start.10 = (f32[5,1,32,1440]{3,2,0,1:T(8,128)S(1)}, f32[5,1,32,1440]{3,2,0,1:T(8,128)S(1)}, u32[]{:S(2)}, u32[]{:S(2)}) collective-permute-start(f32[5,1,32,1440]{3,2,0,1:T(8,128)S(1)} %broadcast_select_fusion.5), channel_id=1, source_target_pairs={{0,4},{4,8},{8,12},{12,16},{16,20},{20,24},{24,28},{28,0},{1,5},{5... | collective-permute-start | bytes 2764808 | tf_op jit(solution)/shard_map/ppermute | solution.py:15
  293.3 5.0 %copy-start.6 = (f32[32]{0:T(128)S(1)}, f32[32]{0:T(128)}, u32[]{:S(2)}) copy-start(f32[32]{0:T(128)} %get-tuple-element.61) | copy-start | bytes 388
  294.5 20.3 %all-to-all-start.2 = ((f32[8,20,1440]{2,1,0:T(8,128)}), f32[8,20,1440]{2,1,0:T(8,128)S(1)}, u32[]{:S(2)}, u32[]{:S(2)}) async-start(f32[8,20,1440]{2,1,0:T(8,128)} %all_to_all.59), calls=%async_computation.2 | async-start | bytes 2359296 | tf_op jit(solution)/shard_map/all_to_all | solution.py:152
  321.0 2.8 copy-start.5
  329.4 1.2 copy-start.14
  341.6 2.9 copy-start
  341.6 2.9 copy-start.1
  347.4 23.3 %copy-start.9 = (f32[1,128]{1,0:T(1,128)S(1)}, f32[1,128]{1,0:T(1,128)}, u32[]{:S(2)}) copy-start(f32[1,128]{1,0:T(1,128)} %get-tuple-element.23) | copy-start | bytes 1540
  366.8 5.8 %collective-permute-start.11 = (f32[5,1,2,1440]{3,2,0,1:T(2,128)S(1)}, f32[5,1,2,1440]{3,2,0,1:T(2,128)S(1)}, u32[]{:S(2)}, u32[]{:S(2)}) collective-permute-start(f32[5,1,2,1440]{3,2,0,1:T(2,128)S(1)} %slice.367), channel_id=1, source_target_pairs={{0,1},{1,2},{2,3},{4,5},{5,6},{6,7},{8,9},{9,10},{10,11},{12,13},{... | collective-permute-start | bytes 172808 | tf_op jit(solution)/shard_map/ppermute | solution.py:21
where the time goes:
time: 381 us; the launch traced here: 375 us
  waiting for transfers between devices  234 us (61%)
  matrix products  31.4 us (8%)
  local copies, waits for them, and re-layouts  30.5 us (8%)
  other arithmetic  29.7 us (8%)
  starting transfers between devices  27.9 us (7%)
  blocking collectives  19.2 us (5%)
    ppermute x10, waiting for transfers between devices, passed_along(): lax.ppermute(x, axis, [(i, (i + by) % devices) for i in range(devices)])  183 us
    all_to_all x2, waiting for transfers between devices, body(): whole = lax.all_to_all(flat, 'lon', split_axis=0, concat_axis=1, tiled=True)  31.3 us
    all_to_all x1, blocking collectives, body(): lax.all_to_all(whole, 'lon', split_axis=1, concat_axis=0, tiled=True)  19.2 us
    all_to_all x1, waiting for transfers between devices, body(): lax.all_to_all(whole, 'lon', split_axis=1, concat_axis=0, tiled=True)  16.2 us
    select_n x22, other arithmetic, roll_digits(): values = jnp.where(taken, moved, values)  11.1 us
    ppermute x10, starting transfers between devices, passed_along(): lax.ppermute(x, axis, [(i, (i + by) % devices) for i in range(devices)])  9.47 us
  transfers between devices with their start and end apart: 15, of which 15 were waited for; matrix products, arithmetic and copies ran while one was open for 1% of the time, Pallas kernels for 0%

commit v1 on v0

--- a/solution.py
+++ b/solution.py
@@ -8,6 +8,22 @@
 FB = 128
 SUBS = 2
 REACH = 4
+
+
+def swapped_with_each(shard, axis, split, join):
+    ways, here = (lax.axis_size(axis), lax.axis_index(axis))
+    width = shard.shape[split] // ways
+    shape = list(shard.shape)
+    shape[split] = width
+    height = shape[join]
+    shape[join] = height * ways
+    full = jnp.zeros(shape, shard.dtype)
+    for mask in range(ways):
+        part = lax.dynamic_slice_in_dim(shard, (here ^ mask) * width, width, axis=split)
+        if mask:
+            part = lax.ppermute(part, axis, [(d, d ^ mask) for d in range(ways)])
+        full = lax.dynamic_update_slice_in_dim(full, part, (here ^ mask) * height, axis=join)
+    return full
 
 
 def passed_along(x, axis, by):
@@ -152,7 +168,7 @@
         whole = lax.all_to_all(flat, "lon", split_axis=0, concat_axis=1, tiled=True)
         whole = zonal_fraction(whole, my_rows(fractions)[:, None])
         whole = polar_smooth(whole, row_lats, row_marks, lat_cells, lat_total)
-        blocks = lax.all_to_all(whole, "lon", split_axis=1, concat_axis=0, tiled=True)
+        blocks = swapped_with_each(whole, "lon", 1, 0)
         state = blocks.reshape(n_fields, n_levels, lat_cells, lon_cells)
         state = meridional(state, frac_y[substep], first_row)
     return state

time: 381 us -> 367 us (0.963)
  blocking collectives: 19.2 us -> 0 us
  local copies, waits for them, and re-layouts: 30.5 us -> 39.3 us
  other arithmetic: 29.7 us -> 25 us
    all_to_all x1 -> x0, blocking collectives: 19.2 us -> none  [body(): lax.all_to_all(whole, 'lon', split_axis=1, concat_axis=0, tiled=True)]
    dynamic_update_slice x0 -> x16, local copies, waits for them, and re-layouts: none -> 17.6 us  [swapped_with_each(): lax.dynamic_update_slice_in_dim(full, part, (here ^ mask) * height, axis=...]
    all_to_all x1 -> x0, waiting for transfers between devices: 16.2 us -> none  [body(): lax.all_to_all(whole, 'lon', split_axis=1, concat_axis=0, tiled=True)]
    ppermute x0 -> x14, waiting for transfers between devices: none -> 13.2 us  [swapped_with_each(): part = lax.ppermute(part, axis, [(d, d ^ mask) for d in range(ways)])]
    ppermute x0 -> x14, starting transfers between devices: none -> 8.45 us  [swapped_with_each(): part = lax.ppermute(part, axis, [(d, d ^ mask) for d in range(ways)])]
    select_n x2, other arithmetic: 6.9 us -> 0.83 us  [polar_smooth(): return jnp.where((marks == 1)[:, None], result, whole)]
    div x2 -> x0, local copies, waits for them, and re-layouts: 5.86 us -> none  [polar_smooth(): result = result.reshape(row_count, lon_total) / lon_total]
  transfers between devices with their start and end apart: 15 -> 28, of which waited for: 15 -> 18; matrix products, arithmetic and copies ran while one was open for 1% -> 5% of each run, Pallas kernels for 0% -> 0%
where the time goes in v1:
time: 367 us; the launch traced here: 360 us
  waiting for transfers between devices  233 us (63%)
  local copies, waits for them, and re-layouts  39.3 us (11%)
  starting transfers between devices  31.7 us (9%)
  matrix products  29.5 us (8%)
  other arithmetic  25 us (7%)
    ppermute x10, waiting for transfers between devices, passed_along(): lax.ppermute(x, axis, [(i, (i + by) % devices) for i in range(devices)])  185 us
    all_to_all x2, waiting for transfers between devices, body(): whole = lax.all_to_all(flat, 'lon', split_axis=0, concat_axis=1, tiled=True)  31.9 us
    dynamic_update_slice x16, local copies, waits for them, and re-layouts, swapped_with_each(): lax.dynamic_update_slice_in_dim(full, part, (here ^ mask) * height, axis=...  17.6 us
    ppermute x14, waiting for transfers between devices, swapped_with_each(): part = lax.ppermute(part, axis, [(d, d ^ mask) for d in range(ways)])  13.2 us
    select_n x22, other arithmetic, roll_digits(): values = jnp.where(taken, moved, values)  11.1 us
    ppermute x14, starting transfers between devices, swapped_with_each(): part = lax.ppermute(part, axis, [(d, d ^ mask) for d in range(ways)])  8.45 us
    ppermute x10, starting transfers between devices, passed_along(): lax.ppermute(x, axis, [(i, (i + by) % devices) for i in range(devices)])  8.01 us
    ppermute x2, starting transfers between devices, passed_along_2(): return lax.ppermute(block, axis, route)  7.7 us
  transfers between devices with their start and end apart: 28, of which 18 were waited for; matrix products, arithmetic and copies ran while one was open for 5% of the time, Pallas kernels for 0%

profile of v1, /device:TPU:0, one launch (start us, length us, event | category | flops | bytes accessed | tf_op | source)
XLA Modules:
  0.0 360.5 jit_solution(18100839967813760847)
XLA Ops:
  0.0 3.0 collective-permute-start
  3.0 22.0 %collective-permute-done = f32[5,1,32,1440]{3,2,1,0:T(8,128)S(1)} collective-permute-done((f32[5,1,32,1440]{3,2,1,0:T(8,128)}, f32[5,1,32,1440]{3,2,1,0:T(8,128)S(1)}, u32[]{:S(2)}, u32[]{:S(2)}) %collective-permute-start) | collective-permute-done | bytes 921632 | tf_op jit(solution)/shard_map/ppermute | solution.py:31
  25.7 13.6 %collective-permute-done.1 = f32[5,1,32,1440]{3,2,1,0:T(8,128)S(1)} collective-permute-done((f32[5,1,32,1440]{3,2,1,0:T(8,128)S(1)}, f32[5,1,32,1440]{3,2,1,0:T(8,128)S(1)}, u32[]{:S(2)}, u32[]{:S(2)}) %collective-permute-start.1) | collective-permute-done | bytes 921632 | tf_op jit(solution)/shard_map/ppermute | solution.py:31
  40.4 22.2 %collective-permute-done.2 = f32[5,1,32,1440]{3,2,1,0:T(8,128)S(1)} collective-permute-done((f32[5,1,32,1440]{3,2,1,0:T(8,128)S(1)}, f32[5,1,32,1440]{3,2,1,0:T(8,128)S(1)}, u32[]{:S(2)}, u32[]{:S(2)}) %collective-permute-start.2) | collective-permute-done | bytes 921632 | tf_op jit(solution)/shard_map/ppermute | solution.py:31
  62.8 1.6 collective-permute-start.3
  64.4 19.7 %collective-permute-done.3 = f32[5,1,32,1440]{3,2,1,0:T(8,128)S(1)} collective-permute-done((f32[5,1,32,1440]{3,2,1,0:T(8,128)S(1)}, f32[5,1,32,1440]{3,2,1,0:T(8,128)S(1)}, u32[]{:S(2)}, u32[]{:S(2)}) %collective-permute-start.3) | collective-permute-done | bytes 921632 | tf_op jit(solution)/shard_map/ppermute | solution.py:31
  84.7 14.1 %collective-permute-done.4 = f32[5,1,32,1440]{3,2,1,0:T(8,128)S(1)} collective-permute-done((f32[5,1,32,1440]{3,2,1,0:T(8,128)S(1)}, f32[5,1,32,1440]{3,2,1,0:T(8,128)S(1)}, u32[]{:S(2)}, u32[]{:S(2)}) %collective-permute-start.4) | collective-permute-done | bytes 921632 | tf_op jit(solution)/shard_map/ppermute | solution.py:31
  107.5 3.8 %all-to-all-start = ((f32[8,20,1440]{2,1,0:T(8,128)}), f32[8,20,1440]{2,1,0:T(8,128)S(1)}, u32[]{:S(2)}, u32[]{:S(2)}) async-start(f32[8,20,1440]{2,1,0:T(8,128)} %all_to_all.32), calls=%async_computation | async-start | bytes 2359296 | tf_op jit(solution)/shard_map/all_to_all | solution.py:168
  112.3 15.5 %all-to-all-done = f32[8,20,1440]{2,1,0:T(8,128)S(1)} async-done(((f32[8,20,1440]{2,1,0:T(8,128)}), f32[8,20,1440]{2,1,0:T(8,128)S(1)}, u32[]{:S(2)}, u32[]{:S(2)}) %all-to-all-start) | async-done | bytes 921632 | tf_op jit(solution)/shard_map/all_to_all | solution.py:168
  128.9 1.4 all_to_all.35
  130.9 1.3 pad_maximum_fusion.5
  132.2 2.4 concatenate.843
  135.8 2.3 multiply_subtract_fusion.3
  138.1 1.2 convolution_bitcast_fusion.1
  139.3 1.2 fusion.13
  140.5 1.2 fusion.45
  141.6 1.2 fusion.46
  142.8 1.2 fusion.12
  145.2 1.6 fusion.11
  149.2 1.2 convolution_add_fusion.2
  150.4 1.3 fusion.33
  151.7 1.3 fusion.10
  155.3 1.3 collective-permute-start.7
  158.9 2.5 collective-permute-done.6
  161.5 1.2 dynamic_update_slice.48
  162.7 1.2 dynamic_update_slice.49
  163.9 1.2 dynamic_update_slice.50
  165.1 1.2 dynamic_update_slice.51
  166.4 1.2 dynamic_update_slice.52
  167.6 4.0 %collective-permute-done.9 = f32[20,1440]{1,0:T(8,128)S(1)} collective-permute-done((f32[20,1440]{1,0:T(8,128)S(1)}, f32[20,1440]{1,0:T(8,128)S(1)}, u32[]{:S(2)}, u32[]{:S(2)}) %collective-permute-start.9) | collective-permute-done | bytes 115232 | tf_op jit(solution)/shard_map/ppermute | solution.py:24
  174.5 3.3 collective-permute-start.12
  177.9 1.8 collective-permute-done.12
  180.3 1.3 collective-permute-start.13
  181.5 22.0 %collective-permute-done.13 = f32[5,1,32,1440]{3,2,0,1:T(8,128)S(1)} collective-permute-done((f32[5,1,32,1440]{3,2,0,1:T(8,128)S(1)}, f32[5,1,32,1440]{3,2,0,1:T(8,128)S(1)}, u32[]{:S(2)}, u32[]{:S(2)}) %collective-permute-start.13) | collective-permute-done | bytes 921632 | tf_op jit(solution)/shard_map/ppermute | solution.py:31
  203.5 14.4 %collective-permute-done.14 = f32[5,1,32,1440]{3,2,0,1:T(8,128)S(1)} collective-permute-done((f32[5,1,32,1440]{3,2,0,1:T(8,128)S(1)}, f32[5,1,32,1440]{3,2,0,1:T(8,128)S(1)}, u32[]{:S(2)}, u32[]{:S(2)}) %collective-permute-start.14) | collective-permute-done | bytes 921632 | tf_op jit(solution)/shard_map/ppermute | solution.py:31
  218.6 22.2 %collective-permute-done.15 = f32[5,1,32,1440]{3,2,0,1:T(8,128)S(1)} collective-permute-done((f32[5,1,32,1440]{3,2,0,1:T(8,128)S(1)}, f32[5,1,32,1440]{3,2,0,1:T(8,128)S(1)}, u32[]{:S(2)}, u32[]{:S(2)}) %collective-permute-start.15) | collective-permute-done | bytes 921632 | tf_op jit(solution)/shard_map/ppermute | solution.py:31
  241.6 20.3 %collective-permute-done.16 = f32[5,1,32,1440]{3,2,0,1:T(8,128)S(1)} collective-permute-done((f32[5,1,32,1440]{3,2,0,1:T(8,128)S(1)}, f32[5,1,32,1440]{3,2,0,1:T(8,128)S(1)}, u32[]{:S(2)}, u32[]{:S(2)}) %collective-permute-start.16) | collective-permute-done | bytes 921632 | tf_op jit(solution)/shard_map/ppermute | solution.py:31
  262.4 14.3 %collective-permute-done.17 = f32[5,1,32,1440]{3,2,0,1:T(8,128)S(1)} collective-permute-done((f32[5,1,32,1440]{3,2,0,1:T(8,128)S(1)}, f32[5,1,32,1440]{3,2,0,1:T(8,128)S(1)}, u32[]{:S(2)}, u32[]{:S(2)}) %collective-permute-start.17) | collective-permute-done | bytes 921632 | tf_op jit(solution)/shard_map/ppermute | solution.py:31
  285.4 3.8 %all-to-all-start.1 = ((f32[8,20,1440]{2,1,0:T(8,128)}), f32[8,20,1440]{2,1,0:T(8,128)S(1)}, u32[]{:S(2)}, u32[]{:S(2)}) async-start(f32[8,20,1440]{2,1,0:T(8,128)} %all_to_all.37), calls=%async_computation.1 | async-start | bytes 2359296 | tf_op jit(solution)/shard_map/all_to_all | solution.py:168
  289.3 16.4 %all-to-all-done.1 = f32[8,20,1440]{2,1,0:T(8,128)S(1)} async-done(((f32[8,20,1440]{2,1,0:T(8,128)}), f32[8,20,1440]{2,1,0:T(8,128)S(1)}, u32[]{:S(2)}, u32[]{:S(2)}) %all-to-all-start.1) | async-done | bytes 921632 | tf_op jit(solution)/shard_map/all_to_all | solution.py:168
  306.8 1.4 all_to_all.40
  308.8 1.3 pad_maximum_fusion.7
  310.1 2.4 concatenate.861
  313.7 2.3 multiply_subtract_fusion.1
  316.0 1.2 convolution_bitcast_fusion
  317.2 1.2 fusion.8
  318.4 1.2 fusion.47
  319.5 1.2 fusion.48
  320.7 1.2 fusion.7
  323.1 1.2 fusion.6
  324.3 1.4 fusion.60
  326.9 1.2 convolution_add_fusion
  328.1 1.3 fusion.26
  329.4 1.3 fusion.5
  333.0 1.3 collective-permute-start.20
  336.6 2.6 collective-permute-done.19
  339.3 1.2 dynamic_update_slice.56
  340.5 1.2 dynamic_update_slice.57
  341.7 1.2 dynamic_update_slice.58
  342.9 1.2 dynamic_update_slice.59
  344.1 1.2 dynamic_update_slice.60
  345.3 4.0 %collective-permute-done.22 = f32[20,1440]{1,0:T(8,128)S(1)} collective-permute-done((f32[20,1440]{1,0:T(8,128)S(1)}, f32[20,1440]{1,0:T(8,128)S(1)}, u32[]{:S(2)}, u32[]{:S(2)}) %collective-permute-start.22) | collective-permute-done | bytes 115232 | tf_op jit(solution)/shard_map/ppermute | solution.py:24
  352.2 4.4 %collective-permute-start.25 = (f32[5,1,2,1440]{3,2,1,0:T(2,128)S(1)}, f32[5,1,2,1440]{3,2,1,0:T(2,128)S(1)}, u32[]{:S(2)}, u32[]{:S(2)}) collective-permute-start(f32[5,1,2,1440]{3,2,1,0:T(2,128)S(1)} %slice.367), channel_id=1, source_target_pairs={{0,1},{1,2},{2,3},{4,5},{5,6},{6,7},{8,9},{9,10},{10,11},{12,13},{... | collective-permute-start | bytes 172808 | tf_op jit(solution)/shard_map/ppermute | solution.py:37
  356.8 1.8 collective-permute-done.25
  (165 shorter events, 51.4 us)
Async XLA Ops:
  0.0 24.9 %collective-permute-start = (f32[5,1,32,1440]{3,2,1,0:T(8,128)}, f32[5,1,32,1440]{3,2,1,0:T(8,128)S(1)}, u32[]{:S(2)}, u32[]{:S(2)}) collective-permute-start(f32[5,1,32,1440]{3,2,1,0:T(8,128)} %param.5), channel_id=1, source_target_pairs={{0,16},{4,20},{8,24},{12,28},{16,0},{20,4},{24,8},{28,12},{1,17},{... | collective-permute-start | bytes 2764808 | tf_op jit(solution)/shard_map/ppermute | solution.py:31
  24.9 14.4 %collective-permute-start.1 = (f32[5,1,32,1440]{3,2,1,0:T(8,128)S(1)}, f32[5,1,32,1440]{3,2,1,0:T(8,128)S(1)}, u32[]{:S(2)}, u32[]{:S(2)}) collective-permute-start(f32[5,1,32,1440]{3,2,1,0:T(8,128)S(1)} %collective-permute-done), channel_id=1, source_target_pairs={{0,4},{4,8},{8,12},{12,16},{16,20},{20,24},{24,28},{28,0},{1,5},{5... | collective-permute-start | bytes 2764808 | tf_op jit(solution)/shard_map/ppermute | solution.py:31
  39.6 23.1 %collective-permute-start.2 = (f32[5,1,32,1440]{3,2,1,0:T(8,128)S(1)}, f32[5,1,32,1440]{3,2,1,0:T(8,128)S(1)}, u32[]{:S(2)}, u32[]{:S(2)}) collective-permute-start(f32[5,1,32,1440]{3,2,1,0:T(8,128)S(1)} %broadcast_select_fusion), channel_id=1, source_target_pairs={{0,8},{4,12},{8,16},{12,20},{16,24},{20,28},{24,0},{28,4},{1,9},{5... | collective-permute-start | bytes 2764808 | tf_op jit(solution)/shard_map/ppermute | solution.py:31
  62.8 21.5 %copy-start.2 = (s32[128]{0:T(128)S(1)}, s32[128]{0:T(128)}, u32[]{:S(2)}) copy-start(s32[128]{0:T(128)} %param.9) | copy-start | bytes 1540
  62.8 21.6 %copy-start = (f32[2,1,128]{2,1,0:T(1,128)S(1)}, f32[2,1,128]{2,1,0:T(1,128)}, u32[]{:S(2)}) copy-start(f32[2,1,128]{2,1,0:T(1,128)} %param.6) | copy-start | bytes 3076
  62.8 21.3 %collective-permute-start.3 = (f32[5,1,32,1440]{3,2,1,0:T(8,128)S(1)}, f32[5,1,32,1440]{3,2,1,0:T(8,128)S(1)}, u32[]{:S(2)}, u32[]{:S(2)}) collective-permute-start(f32[5,1,32,1440]{3,2,1,0:T(8,128)S(1)} %broadcast_select_fusion.1), channel_id=1, source_target_pairs={{0,16},{4,20},{8,24},{12,28},{16,0},{20,4},{24,8},{28,12},{1,17},{... | collective-permute-start | bytes 2764808 | tf_op jit(solution)/shard_map/ppermute | solution.py:31
  84.3 14.5 %collective-permute-start.4 = (f32[5,1,32,1440]{3,2,1,0:T(8,128)S(1)}, f32[5,1,32,1440]{3,2,1,0:T(8,128)S(1)}, u32[]{:S(2)}, u32[]{:S(2)}) collective-permute-start(f32[5,1,32,1440]{3,2,1,0:T(8,128)S(1)} %broadcast_select_fusion.2), channel_id=1, source_target_pairs={{0,4},{4,8},{8,12},{12,16},{16,20},{20,24},{24,28},{28,0},{1,5},{5... | collective-permute-start | bytes 2764808 | tf_op jit(solution)/shard_map/ppermute | solution.py:31
  107.5 20.3 %all-to-all-start = ((f32[8,20,1440]{2,1,0:T(8,128)}), f32[8,20,1440]{2,1,0:T(8,128)S(1)}, u32[]{:S(2)}, u32[]{:S(2)}) async-start(f32[8,20,1440]{2,1,0:T(8,128)} %all_to_all.32), calls=%async_computation | async-start | bytes 2359296 | tf_op jit(solution)/shard_map/all_to_all | solution.py:168
  154.2 7.2 %copy-start.1 = (f32[2,1,128]{2,1,0:T(1,128)S(1)}, f32[2,1,128]{2,1,0:T(1,128)}, u32[]{:S(2)}) copy-start(f32[2,1,128]{2,1,0:T(1,128)} %param.7) | copy-start | bytes 3076
  154.6 3.6 %collective-permute-start.5 = (f32[20,1440]{1,0:T(8,128)S(1)}, f32[20,1440]{1,0:T(8,128)S(1)}, u32[]{:S(2)}, u32[]{:S(2)}) collective-permute-start(f32[20,1440]{1,0:T(8,128)S(1)} %get-tuple-element.37), channel_id=1, source_target_pairs={{0,4},{4,0},{8,12},{12,8},{16,20},{20,16},{24,28},{28,24},{1,5},{5... | collective-permute-start | bytes 345608 | tf_op jit(solution)/shard_map/ppermute | solution.py:24
  154.7 6.7 %collective-permute-start.6 = (f32[20,1440]{1,0:T(8,128)S(1)}, f32[20,1440]{1,0:T(8,128)S(1)}, u32[]{:S(2)}, u32[]{:S(2)}) collective-permute-start(f32[20,1440]{1,0:T(8,128)S(1)} %get-tuple-element.36), channel_id=1, source_target_pairs={{0,8},{4,12},{8,0},{12,4},{16,24},{20,28},{24,16},{28,20},{1,9},{5... | collective-permute-start | bytes 345608 | tf_op jit(solution)/shard_map/ppermute | solution.py:24
  155.3 9.8 %collective-permute-start.7 = (f32[20,1440]{1,0:T(8,128)S(1)}, f32[20,1440]{1,0:T(8,128)S(1)}, u32[]{:S(2)}, u32[]{:S(2)}) collective-permute-start(f32[20,1440]{1,0:T(8,128)S(1)} %get-tuple-element.35), channel_id=1, source_target_pairs={{0,12},{4,8},{8,4},{12,0},{16,28},{20,24},{24,20},{28,16},{1,13},{... | collective-permute-start | bytes 345608 | tf_op jit(solution)/shard_map/ppermute | solution.py:24
  156.6 9.8 %collective-permute-start.8 = (f32[20,1440]{1,0:T(8,128)S(1)}, f32[20,1440]{1,0:T(8,128)S(1)}, u32[]{:S(2)}, u32[]{:S(2)}) collective-permute-start(f32[20,1440]{1,0:T(8,128)S(1)} %get-tuple-element.34), channel_id=1, source_target_pairs={{0,16},{4,20},{8,24},{12,28},{16,0},{20,4},{24,8},{28,12},{1,17},{... | collective-permute-start | bytes 345608 | tf_op jit(solution)/shard_map/ppermute | solution.py:24
  157.1 14.5 %collective-permute-start.9 = (f32[20,1440]{1,0:T(8,128)S(1)}, f32[20,1440]{1,0:T(8,128)S(1)}, u32[]{:S(2)}, u32[]{:S(2)}) collective-permute-start(f32[20,1440]{1,0:T(8,128)S(1)} %get-tuple-element.33), channel_id=1, source_target_pairs={{0,20},{4,16},{8,28},{12,24},{16,4},{20,0},{24,12},{28,8},{1,21},{... | collective-permute-start | bytes 345608 | tf_op jit(solution)/shard_map/ppermute | solution.py:24
  158.3 14.4 %collective-permute-start.10 = (f32[20,1440]{1,0:T(8,128)S(1)}, f32[20,1440]{1,0:T(8,128)S(1)}, u32[]{:S(2)}, u32[]{:S(2)}) collective-permute-start(f32[20,1440]{1,0:T(8,128)S(1)} %get-tuple-element.32), channel_id=1, source_target_pairs={{0,24},{4,28},{8,16},{12,20},{16,8},{20,12},{24,0},{28,4},{1,25},{... | collective-permute-start | bytes 345608 | tf_op jit(solution)/shard_map/ppermute | solution.py:24
  161.4 12.3 %collective-permute-start.11 = (f32[20,1440]{1,0:T(8,128)S(1)}, f32[20,1440]{1,0:T(8,128)S(1)}, u32[]{:S(2)}, u32[]{:S(2)}) collective-permute-start(f32[20,1440]{1,0:T(8,128)S(1)} %get-tuple-element.31), channel_id=1, source_target_pairs={{0,28},{4,24},{8,20},{12,16},{16,12},{20,8},{24,4},{28,0},{1,29},{... | collective-permute-start | bytes 345608 | tf_op jit(solution)/shard_map/ppermute | solution.py:24
  174.5 5.1 %collective-permute-start.12 = (f32[5,1,2,1440]{3,2,0,1:T(2,128)S(1)}, f32[5,1,2,1440]{3,2,0,1:T(2,128)S(1)}, u32[]{:S(2)}, u32[]{:S(2)}) collective-permute-start(f32[5,1,2,1440]{3,2,0,1:T(2,128)S(1)} %slice.334), channel_id=1, source_target_pairs={{0,1},{1,2},{2,3},{4,5},{5,6},{6,7},{8,9},{9,10},{10,11},{12,13},{... | collective-permute-start | bytes 172808 | tf_op jit(solution)/shard_map/ppermute | solution.py:37
  180.3 23.2 %collective-permute-start.13 = (f32[5,1,32,1440]{3,2,0,1:T(8,128)S(1)}, f32[5,1,32,1440]{3,2,0,1:T(8,128)S(1)}, u32[]{:S(2)}, u32[]{:S(2)}) collective-permute-start(f32[5,1,32,1440]{3,2,0,1:T(8,128)S(1)} %slice_subtract_fusion.1), channel_id=1, source_target_pairs={{0,16},{4,20},{8,24},{12,28},{16,0},{20,4},{24,8},{28,12},{1,17},{... | collective-permute-start | bytes 2764808 | tf_op jit(solution)/shard_map/ppermute | solution.py:31
  203.5 14.4 %collective-permute-start.14 = (f32[5,1,32,1440]{3,2,0,1:T(8,128)S(1)}, f32[5,1,32,1440]{3,2,0,1:T(8,128)S(1)}, u32[]{:S(2)}, u32[]{:S(2)}) collective-permute-start(f32[5,1,32,1440]{3,2,0,1:T(8,128)S(1)} %collective-permute-done.13), channel_id=1, source_target_pairs={{0,4},{4,8},{8,12},{12,16},{16,20},{20,24},{24,28},{28,0},{1,5},{5... | collective-permute-start | bytes 2764808 | tf_op jit(solution)/shard_map/ppermute | solution.py:31
  218.1 22.6 %collective-permute-start.15 = (f32[5,1,32,1440]{3,2,0,1:T(8,128)S(1)}, f32[5,1,32,1440]{3,2,0,1:T(8,128)S(1)}, u32[]{:S(2)}, u32[]{:S(2)}) collective-permute-start(f32[5,1,32,1440]{3,2,0,1:T(8,128)S(1)} %broadcast_select_fusion.3), channel_id=1, source_target_pairs={{0,8},{4,12},{8,16},{12,20},{16,24},{20,28},{24,0},{28,4},{1,9},{5... | collective-permute-start | bytes 2764808 | tf_op jit(solution)/shard_map/ppermute | solution.py:31
  241.0 20.9 %collective-permute-start.16 = (f32[5,1,32,1440]{3,2,0,1:T(8,128)S(1)}, f32[5,1,32,1440]{3,2,0,1:T(8,128)S(1)}, u32[]{:S(2)}, u32[]{:S(2)}) collective-permute-start(f32[5,1,32,1440]{3,2,0,1:T(8,128)S(1)} %broadcast_select_fusion.4), channel_id=1, source_target_pairs={{0,16},{4,20},{8,24},{12,28},{16,0},{20,4},{24,8},{28,12},{1,17},{... | collective-permute-start | bytes 2764808 | tf_op jit(solution)/shard_map/ppermute | solution.py:31
  262.0 14.6 %collective-permute-start.17 = (f32[5,1,32,1440]{3,2,0,1:T(8,128)S(1)}, f32[5,1,32,1440]{3,2,0,1:T(8,128)S(1)}, u32[]{:S(2)}, u32[]{:S(2)}) collective-permute-start(f32[5,1,32,1440]{3,2,0,1:T(8,128)S(1)} %broadcast_select_fusion.5), channel_id=1, source_target_pairs={{0,4},{4,8},{8,12},{12,16},{16,20},{20,24},{24,28},{28,0},{1,5},{5... | collective-permute-start | bytes 2764808 | tf_op jit(solution)/shard_map/ppermute | solution.py:31
  285.4 20.3 %all-to-all-start.1 = ((f32[8,20,1440]{2,1,0:T(8,128)}), f32[8,20,1440]{2,1,0:T(8,128)S(1)}, u32[]{:S(2)}, u32[]{:S(2)}) async-start(f32[8,20,1440]{2,1,0:T(8,128)} %all_to_all.37), calls=%async_computation.1 | async-start | bytes 2359296 | tf_op jit(solution)/shard_map/all_to_all | solution.py:168
  332.4 3.6 %collective-permute-start.18 = (f32[20,1440]{1,0:T(8,128)S(1)}, f32[20,1440]{1,0:T(8,128)S(1)}, u32[]{:S(2)}, u32[]{:S(2)}) collective-permute-start(f32[20,1440]{1,0:T(8,128)S(1)} %get-tuple-element.29), channel_id=1, source_target_pairs={{0,4},{4,0},{8,12},{12,8},{16,20},{20,16},{24,28},{28,24},{1,5},{5... | collective-permute-start | bytes 345608 | tf_op jit(solution)/shard_map/ppermute | solution.py:24
  332.5 6.7 %collective-permute-start.19 = (f32[20,1440]{1,0:T(8,128)S(1)}, f32[20,1440]{1,0:T(8,128)S(1)}, u32[]{:S(2)}, u32[]{:S(2)}) collective-permute-start(f32[20,1440]{1,0:T(8,128)S(1)} %get-tuple-element.28), channel_id=1, source_target_pairs={{0,8},{4,12},{8,0},{12,4},{16,24},{20,28},{24,16},{28,20},{1,9},{5... | collective-permute-start | bytes 345608 | tf_op jit(solution)/shard_map/ppermute | solution.py:24
  333.0 9.8 %collective-permute-start.20 = (f32[20,1440]{1,0:T(8,128)S(1)}, f32[20,1440]{1,0:T(8,128)S(1)}, u32[]{:S(2)}, u32[]{:S(2)}) collective-permute-start(f32[20,1440]{1,0:T(8,128)S(1)} %get-tuple-element.27), channel_id=1, source_target_pairs={{0,12},{4,8},{8,4},{12,0},{16,28},{20,24},{24,20},{28,16},{1,13},{... | collective-permute-start | bytes 345608 | tf_op jit(solution)/shard_map/ppermute | solution.py:24
  334.3 9.8 %collective-permute-start.21 = (f32[20,1440]{1,0:T(8,128)S(1)}, f32[20,1440]{1,0:T(8,128)S(1)}, u32[]{:S(2)}, u32[]{:S(2)}) collective-permute-start(f32[20,1440]{1,0:T(8,128)S(1)} %get-tuple-element.26), channel_id=1, source_target_pairs={{0,16},{4,20},{8,24},{12,28},{16,0},{20,4},{24,8},{28,12},{1,17},{... | collective-permute-start | bytes 345608 | tf_op jit(solution)/shard_map/ppermute | solution.py:24
  334.9 14.5 %collective-permute-start.22 = (f32[20,1440]{1,0:T(8,128)S(1)}, f32[20,1440]{1,0:T(8,128)S(1)}, u32[]{:S(2)}, u32[]{:S(2)}) collective-permute-start(f32[20,1440]{1,0:T(8,128)S(1)} %get-tuple-element.25), channel_id=1, source_target_pairs={{0,20},{4,16},{8,28},{12,24},{16,4},{20,0},{24,12},{28,8},{1,21},{... | collective-permute-start | bytes 345608 | tf_op jit(solution)/shard_map/ppermute | solution.py:24
  336.0 14.4 %collective-permute-start.23 = (f32[20,1440]{1,0:T(8,128)S(1)}, f32[20,1440]{1,0:T(8,128)S(1)}, u32[]{:S(2)}, u32[]{:S(2)}) collective-permute-start(f32[20,1440]{1,0:T(8,128)S(1)} %get-tuple-element.24), channel_id=1, source_target_pairs={{0,24},{4,28},{8,16},{12,20},{16,8},{20,12},{24,0},{28,4},{1,25},{... | collective-permute-start | bytes 345608 | tf_op jit(solution)/shard_map/ppermute | solution.py:24
  339.2 12.3 %collective-permute-start.24 = (f32[20,1440]{1,0:T(8,128)S(1)}, f32[20,1440]{1,0:T(8,128)S(1)}, u32[]{:S(2)}, u32[]{:S(2)}) collective-permute-start(f32[20,1440]{1,0:T(8,128)S(1)} %get-tuple-element.23), channel_id=1, source_target_pairs={{0,28},{4,24},{8,20},{12,16},{16,12},{20,8},{24,4},{28,0},{1,29},{... | collective-permute-start | bytes 345608 | tf_op jit(solution)/shard_map/ppermute | solution.py:24
  352.2 6.3 %collective-permute-start.25 = (f32[5,1,2,1440]{3,2,1,0:T(2,128)S(1)}, f32[5,1,2,1440]{3,2,1,0:T(2,128)S(1)}, u32[]{:S(2)}, u32[]{:S(2)}) collective-permute-start(f32[5,1,2,1440]{3,2,1,0:T(2,128)S(1)} %slice.367), channel_id=1, source_target_pairs={{0,1},{1,2},{2,3},{4,5},{5,6},{6,7},{8,9},{9,10},{10,11},{12,13},{... | collective-permute-start | bytes 172808 | tf_op jit(solution)/shard_map/ppermute | solution.py:37
